TPU v7x, 512 devices: a whole 4x8x8 slice. The times are simulated.
512 devices in a mesh: row: 16 (over y_hi, x), blk: 32 (over y_lo, z, core).
Axes of the slice: x: 4, y: 8 (y_hi: 4, y_lo: 2; y = y_hi * 2 + y_lo), z: 8, core: 2. Of those that a mesh axis runs over, the one named last changes fastest.
Arguments:
- features: bfloat16 [131072, 512], P(('row', 'blk')), may hold values from -6 to 6
- edge_tiles: bfloat16 [16, 32, 48, 128, 128], P('row', 'blk'), may hold values from 0 to 1
- tile_src: int32 [16, 32, 48], P('row', 'blk'), may hold values from 0 to 63, as said below
- tile_dst: int32 [16, 32, 48], P('row', 'blk'), may hold values from 0 to 31
- tile_count: int32 [16, 32], P('row', 'blk'), may hold values from 9 to 48, as said below
- weight: bfloat16 [1024, 512], replicated, may hold values from -0.25 to 0.25
- out_bias: float32 [512], replicated, may hold values from -3 to 3
Outputs:
- exposure: bfloat16 [131072, 512], P(('row', 'blk'))
Inputs may be any that keep to these rules, and one draw needn't show every extreme that they name: `tile_count`: live slots of a device; the busiest device has all 48. `tile_src`: the live entries of each device ascend; source block s lies at loop position s // 2, which may be any position of the closed loop of 32 positions.
All inputs are finite; a program needn't handle non-finite values.
Results may differ from a plain program's by a relative error of at most 0.006.
Values may be sent and summed in bfloat16 or wider, within the bound.
No kernel may reach another device: no remote copies, remote signals or barrier semaphores. Data moves between devices by JAX's collectives and lax.ppermute only.
A program may use at most 128 MiB of HBM per device.

v0:
```python
import jax
import jax.numpy as jnp
from jax import lax
from jax.sharding import PartitionSpec as P


def accumulate(table, block_of, tiles_here, target_ids, live_slot, dest_blocks):
    slot_total = tiles_here.shape[0]
    tile_width = tiles_here.shape[-1]
    feat_width = table.shape[1]
    table_blocks = table.reshape(-1, tile_width, feat_width)
    source_total = table_blocks.shape[0]
    step_size = 16
    rounds = slot_total // step_size
    source_ids = jnp.arange(source_total, dtype=jnp.int32)
    dest_ids = jnp.arange(dest_blocks, dtype=jnp.int32)

    def one_round(index, totals):
        first = index * step_size
        tiles = lax.dynamic_slice_in_dim(tiles_here, first, step_size, 0)
        blocks = lax.dynamic_slice_in_dim(block_of, first, step_size, 0)
        targets = lax.dynamic_slice_in_dim(target_ids, first, step_size, 0)
        live = lax.dynamic_slice_in_dim(live_slot, first, step_size, 0)
        one_hot = (blocks[:, None] == source_ids[None, :]).astype(jnp.bfloat16)
        picked = jnp.einsum(
            "tk,kif->tif", one_hot, table_blocks, preferred_element_type=jnp.float32
        ).astype(jnp.bfloat16)
        products = jnp.einsum("tij,tjf->tif", tiles, picked, preferred_element_type=jnp.float32)
        selector = ((targets[None, :] == dest_ids[:, None]) & live[None, :]).astype(jnp.float32)
        return totals + jnp.einsum(
            "qt,tif->qif", selector, products, precision=lax.Precision.HIGHEST
        )

    empty = jnp.zeros((dest_blocks, tile_width, feat_width), jnp.float32)
    return lax.fori_loop(0, rounds, one_round, empty)


def per_device(features, edge_tiles, tile_src, tile_dst, tile_count, weight, out_bias):
    tiles_here = edge_tiles[0, 0]
    source_ids = tile_src[0, 0]
    target_ids = tile_dst[0, 0]
    live_count = tile_count[0, 0]
    slot_total = tiles_here.shape[0]
    tile_width = tiles_here.shape[-1]
    node_rows = features.shape[0]
    feat_width = features.shape[1]
    group_count = lax.axis_size("row")
    dest_blocks = group_count * node_rows // tile_width
    slot_ids = jnp.arange(slot_total, dtype=jnp.int32)
    live_slot = slot_ids < live_count
    table = lax.all_gather(features, "blk", axis=0, tiled=True)
    totals = accumulate(table, source_ids, tiles_here, target_ids, live_slot, dest_blocks).reshape(
        -1, feat_width
    )
    row_sums = jnp.sum(tiles_here, axis=2, dtype=jnp.float32)
    block_ids = jnp.arange(dest_blocks, dtype=jnp.int32)
    selector = ((target_ids[None, :] == block_ids[:, None]) & live_slot[None, :]).astype(
        jnp.float32
    )
    degree_part = jnp.dot(selector, row_sums, precision=lax.Precision.HIGHEST).reshape(-1)
    aggregate, degree = (
        lax.psum_scatter(
            totals.astype(jnp.bfloat16), "row", scatter_dimension=0, tiled=True
        ).astype(jnp.float32),
        lax.psum_scatter(
            degree_part.astype(jnp.bfloat16), "row", scatter_dimension=0, tiled=True
        ).astype(jnp.float32),
    )
    neighbor_mean = (aggregate / jnp.maximum(degree, 1.0)[:, None]).astype(jnp.bfloat16)
    joined = jnp.concatenate([features, neighbor_mean], axis=1)
    mixed = jnp.dot(joined, weight, preferred_element_type=jnp.float32) + out_bias
    return jax.nn.relu(mixed).astype(jnp.bfloat16)


def solution(mesh):
    in_specs = (
        P(("row", "blk"), None),
        P("row", "blk", None, None, None),
        P("row", "blk", None),
        P("row", "blk", None),
        P("row", "blk"),
        P(),
        P(),
    )
    out_specs = P(("row", "blk"), None)
    return jax.shard_map(
        per_device, mesh=mesh, in_specs=in_specs, out_specs=out_specs, check_vma=False
    )
```

profile of v0, /device:TPU:6, one launch (start us, length us, event | category | flops | bytes accessed | tf_op | source)
XLA Modules:
  0.0 281.0 jit_solution(13187244647152647785)
XLA Ops:
  6.5 0.7 all-gather.2.cloned.1.call-update
  7.3 0.0 reduce-scatter.2.cloned.1.call-start
  8.0 81.0 %all-gather.2.cloned.1.call-done = bf16[8192,512]{1,0:T(8,128)(2,1)} async-done(((bf16[256,512]{1,0:T(8,128)(2,1)}), bf16[8192,512]{1,0:T(8,128)(2,1)}) %all-gather.2.cloned.1.call-update) | async-done | bytes 8388624 | tf_op jit(solution)/shard_map/all_gather | solution.py:51
  89.0 11.4 %copy.14 = bf16[64,128,512]{2,0,1:T(8,128)(2,1)} copy(bf16[64,128,512]{2,1,0:T(8,128)(2,1)} %bitcast.29) | data formatting | bytes 16777216
  100.5 61.2 %while.14 = (s32[]{:T(128)}, f32[32,128,512]{2,0,1:T(8,128)}, s32[48]{0:T(128)S(1)}, pred[48]{0:T(512)(128)(4,1)S(1)}, bf16[48,128,128]{2,1,0:T(8,128)(2,1)S(1)}...) while((s32[]{:T(128)}, f32[32,128,512]{2,0,1:T(8,128)}, ...), condition=%wide.region_1.0_spmd.clone, body=%wide.region_0.0_spmd.clone.sunk | while | flops 810551296 | bytes 38273636 | solution.py:35
  100.7 0.1 dynamic_slice.39
  100.7 4.6 %convolution_convert_fusion.3 = bf16[16,128,512]{2,0,1:T(8,128)(2,1)S(1)} fusion(bf16[64,128,512]{2,0,1:T(8,128)(2,1)} %get-tuple-element.280, s32[16]{0:T(128)S(1)} %dynamic_slice.39), kind=kOutput, calls=%fused_computation.7.clone.1 | convolution fusion | flops 135267328 | bytes 10485824 | tf_op jit(solution)/shard_map/while/body/eval_jaxpr/tk,kif->tif/dot_general | solution.py:25
  105.4 4.6 %fusion.47 = f32[16,128,512]{2,1,0:T(8,128)} fusion(bf16[16,128,512]{2,0,1:T(8,128)(2,1)S(1)} %convolution_convert_fusion.3, bf16[48,128,128]{2,1,0:T(8,128)(2,1)S(1)} %get-tuple-element.278, s32[]{:T(128)S(6)} %select_n.12), kind=kOutput, calls=%fused_computation.5.clone.1 | convolution fusion | flops 268435456 | bytes 6815748 | tf_op jit(solution)/shard_map/while/body/eval_jaxpr/tij,tjf->tif/dot_general | solution.py:28
  110.0 0.1 dynamic_slice.40
  110.0 0.1 dynamic_slice.41
  110.1 10.1 %select_add_fusion.2 = f32[32,128,512]{2,0,1:T(8,128)} fusion(f32[32,128,512]{2,0,1:T(8,128)} %get-tuple-element.264, pred[]{:T(512)S(6)} %compare.3, f32[16,128,512]{2,1,0:T(8,128)} %fusion.47, s32[16]{0:T(128)S(1)} %dynamic_slice.40, pred[16]{0:T(512)(128)(4,1)S(1)} %dynamic_slice.41), kind=kOutput, calls=%fused_computation.2.clone.1 | convolution fusion | flops 406848512 | bytes 20971600 | tf_op jit(solution)/shard_map/while/body/eval_jaxpr/qt,tif->qif/dot_general | solution.py:30
  120.2 0.1 dynamic_slice.39
  120.2 4.6 %convolution_convert_fusion.3 = bf16[16,128,512]{2,0,1:T(8,128)(2,1)S(1)} fusion(bf16[64,128,512]{2,0,1:T(8,128)(2,1)} %get-tuple-element.280, s32[16]{0:T(128)S(1)} %dynamic_slice.39), kind=kOutput, calls=%fused_computation.7.clone.1 | convolution fusion | flops 135267328 | bytes 10485824 | tf_op jit(solution)/shard_map/while/body/eval_jaxpr/tk,kif->tif/dot_general | solution.py:25
  124.9 4.6 %fusion.47 = f32[16,128,512]{2,1,0:T(8,128)} fusion(bf16[16,128,512]{2,0,1:T(8,128)(2,1)S(1)} %convolution_convert_fusion.3, bf16[48,128,128]{2,1,0:T(8,128)(2,1)S(1)} %get-tuple-element.278, s32[]{:T(128)S(6)} %select_n.12), kind=kOutput, calls=%fused_computation.5.clone.1 | convolution fusion | flops 268435456 | bytes 6815748 | tf_op jit(solution)/shard_map/while/body/eval_jaxpr/tij,tjf->tif/dot_general | solution.py:28
  129.5 0.1 dynamic_slice.40
  129.5 0.1 dynamic_slice.41
  129.6 11.3 %select_add_fusion.2 = f32[32,128,512]{2,0,1:T(8,128)} fusion(f32[32,128,512]{2,0,1:T(8,128)} %get-tuple-element.264, pred[]{:T(512)S(6)} %compare.3, f32[16,128,512]{2,1,0:T(8,128)} %fusion.47, s32[16]{0:T(128)S(1)} %dynamic_slice.40, pred[16]{0:T(512)(128)(4,1)S(1)} %dynamic_slice.41), kind=kOutput, calls=%fused_computation.2.clone.1 | convolution fusion | flops 406848512 | bytes 20971600 | tf_op jit(solution)/shard_map/while/body/eval_jaxpr/qt,tif->qif/dot_general | solution.py:30
  140.9 0.1 dynamic_slice.39
  141.0 4.6 %convolution_convert_fusion.3 = bf16[16,128,512]{2,0,1:T(8,128)(2,1)S(1)} fusion(bf16[64,128,512]{2,0,1:T(8,128)(2,1)} %get-tuple-element.280, s32[16]{0:T(128)S(1)} %dynamic_slice.39), kind=kOutput, calls=%fused_computation.7.clone.1 | convolution fusion | flops 135267328 | bytes 10485824 | tf_op jit(solution)/shard_map/while/body/eval_jaxpr/tk,kif->tif/dot_general | solution.py:25
  145.6 4.6 %fusion.47 = f32[16,128,512]{2,1,0:T(8,128)} fusion(bf16[16,128,512]{2,0,1:T(8,128)(2,1)S(1)} %convolution_convert_fusion.3, bf16[48,128,128]{2,1,0:T(8,128)(2,1)S(1)} %get-tuple-element.278, s32[]{:T(128)S(6)} %select_n.12), kind=kOutput, calls=%fused_computation.5.clone.1 | convolution fusion | flops 268435456 | bytes 6815748 | tf_op jit(solution)/shard_map/while/body/eval_jaxpr/tij,tjf->tif/dot_general | solution.py:28
  150.2 0.1 dynamic_slice.40
  150.3 0.1 dynamic_slice.41
  150.3 11.3 %select_add_fusion.2 = f32[32,128,512]{2,0,1:T(8,128)} fusion(f32[32,128,512]{2,0,1:T(8,128)} %get-tuple-element.264, pred[]{:T(512)S(6)} %compare.3, f32[16,128,512]{2,1,0:T(8,128)} %fusion.47, s32[16]{0:T(128)S(1)} %dynamic_slice.40, pred[16]{0:T(512)(128)(4,1)S(1)} %dynamic_slice.41), kind=kOutput, calls=%fused_computation.2.clone.1 | convolution fusion | flops 406848512 | bytes 20971600 | tf_op jit(solution)/shard_map/while/body/eval_jaxpr/qt,tif->qif/dot_general | solution.py:30
  161.6 9.8 %copy.23 = bf16[32,128,512]{2,1,0:T(8,128)(2,1)} copy(f32[32,128,512]{2,0,1:T(8,128)} %get-tuple-element.159) | data formatting | bytes 12582912 | tf_op jit(solution)/shard_map/while | solution.py:35
  171.4 1.3 dynamic-slice
  173.4 0.5 convert_reduce_fusion
  173.9 0.1 fusion.22
  174.0 36.3 %all-reduce = bf16[4096]{0:T(1024)(128)(2,1)S(1)} all-reduce(bf16[4096]{0:T(1024)(128)(2,1)S(1)} %fusion.22), channel_id=3, replica_groups=mesh['row'=16,'blk'=32] {'row'}, use_global_device_ids=true, to_apply=%region_4.0.clone | all-reduce | flops 4096 | bytes 16384
  210.3 0.1 convert_maximum_fusion
  210.4 61.5 %reduce-scatter.2.cloned.1.call-done = bf16[256,512]{1,0:T(8,128)(2,1)} async-done(((bf16[4096,512]{1,0:T(8,128)(2,1)}), bf16[256,512]{1,0:T(8,128)(2,1)}) %reduce-scatter.2.cloned.1.call-update) | async-done | bytes 262160 | tf_op jit(solution)/shard_map/reduce_scatter | solution.py:62
  271.9 1.1 divide_convert_fusion
  273.0 1.1 fusion.21
  (16 shorter events, 0.0 us)
Async XLA Ops:
  6.5 266.4 %copy-start = (bf16[1024,512]{1,0:T(8,128)(2,1)S(1)}, bf16[1024,512]{1,0:T(8,128)(2,1)}, u32[]{:S(2)}) copy-start(bf16[1024,512]{1,0:T(8,128)(2,1)} %param.14) | copy-start | bytes 3145732
  6.5 82.4 %all-gather.2.cloned.1.call-start = ((), (), s32[]{:S(2)}) async-start(), calls=%async_computation.1 | async-start | bytes 8650752 | tf_op jit(solution)/shard_map/all_gather | solution.py:51
  7.3 264.6 %reduce-scatter.2.cloned.1.call-start = ((), (), s32[]{:S(2)}) async-start(), calls=%async_computation.2 | async-start | bytes 4456448 | tf_op jit(solution)/shard_map/reduce_scatter | solution.py:62
  89.0 11.5 %copy-start.1 = (bf16[1,1,48,128,128]{4,3,2,1,0:T(8,128)(2,1)S(1)}, bf16[1,1,48,128,128]{4,3,2,1,0:T(8,128)(2,1)}, u32[]{:S(2)}) copy-start(bf16[1,1,48,128,128]{4,3,2,1,0:T(8,128)(2,1)} %param.10) | copy-start | bytes 4718596
  89.0 11.5 %copy-start.3 = (s32[1,1,48]{2,1,0:T(1,128)S(1)}, s32[1,1,48]{2,1,0:T(1,128)}, u32[]{:S(2)}) copy-start(s32[1,1,48]{2,1,0:T(1,128)} %param.12) | copy-start | bytes 580
  89.0 11.5 %copy-start.5 = (s32[1,1,48]{2,1,0:T(1,128)S(1)}, s32[1,1,48]{2,1,0:T(1,128)}, u32[]{:S(2)}) copy-start(s32[1,1,48]{2,1,0:T(1,128)} %param.11) | copy-start | bytes 580
  171.4 101.6 %copy-start.2 = (bf16[256,512]{1,0:T(8,128)(2,1)S(1)}, bf16[256,512]{1,0:T(8,128)(2,1)}, u32[]{:S(2)}) copy-start(bf16[256,512]{1,0:T(8,128)(2,1)} %param.9) | copy-start | bytes 786436
  171.4 101.6 %copy-start.4 = (f32[512]{0:T(512)S(1)}, f32[512]{0:T(512)}, u32[]{:S(2)}) copy-start(f32[512]{0:T(512)} %param.15) | copy-start | bytes 6148
Sparse Core Ops, SparseCore 0:
  9.5 79.4 all-gather.1
  171.5 100.3 reduce-scatter.1
where the time goes:
time: 282 us; the launch traced here: 281 us
  waiting for transfers between devices  143 us (51%)
  matrix products  61.5 us (22%)
  blocking collectives  36.3 us (13%)
  local copies, waits for them, and re-layouts  23.2 us (8%)
  between operations  14.8 us (5%)
    all_gather x1, waiting for transfers between devices, per_device(): table = lax.all_gather(features, 'blk', axis=0, tiled=True)  81 us
    reduce_scatter x1, waiting for transfers between devices, per_device(): lax.psum_scatter(totals.astype(jnp.bfloat16), 'row', scatter_dimension=0,...  61.5 us
    unnamed x1, blocking collectives  36.3 us
    dot_general x3, matrix products, one_round(): jnp.einsum('qt,tif->qif', selector, products, precision=lax.Precision.HIG...  32.6 us
    dot_general x3, matrix products, one_round(): jnp.einsum('tk,kif->tif', one_hot, table_blocks, preferred_element_type=j...  13.9 us
    dot_general x3, matrix products, one_round(): jnp.einsum('tij,tjf->tif', tiles, picked, preferred_element_type=jnp.floa...  13.7 us
    unnamed x14, local copies, waits for them, and re-layouts  12.8 us
    while x1, local copies, waits for them, and re-layouts, accumulate(): return lax.fori_loop(0, rounds, one_round, empty)  9.77 us
  transfers between devices with their start and end apart: 2, of which 2 were waited for; matrix products, arithmetic and copies ran while one was open for 1% of the time, Pallas kernels for 0%

commit v1 on v0

v1 whole, which is shorter than its diff:
```python
import jax
import jax.numpy as jnp
from jax import lax
from jax.experimental import pallas as pl
from jax.experimental.pallas import tpu as pltpu
from jax.sharding import PartitionSpec as P

UNROLL = 4


def scatter_matmul(table, tiles, source_ids, target_ids, live_count, dest_blocks):
    slot_total, tile_width, unused = tiles.shape
    feat_width = table.shape[-1]

    def kernel(src_ref, dst_ref, count_ref, table_ref, tiles_ref, out_ref, total_ref):
        count = count_ref[0]

        def clear(block, carry):
            total_ref[block] = jnp.zeros((tile_width, feat_width), jnp.float32)
            return carry

        lax.fori_loop(0, dest_blocks, clear, 0)

        def some_slots(index, carry):
            products = []
            for step in range(UNROLL):
                slot = index * UNROLL + step
                products.append(
                    jnp.dot(
                        tiles_ref[slot],
                        table_ref[src_ref[slot]],
                        preferred_element_type=jnp.float32,
                    )
                )
            for step in range(UNROLL):
                slot = index * UNROLL + step
                target = jnp.where(slot < count, dst_ref[slot], dest_blocks)
                total_ref[target] += products[step]
            return carry

        lax.fori_loop(0, pl.cdiv(count, UNROLL), some_slots, 0)

        def round_once(block, carry):
            out_ref[block] = total_ref[block].astype(jnp.bfloat16)
            return carry

        lax.fori_loop(0, dest_blocks, round_once, 0)

    smem = pl.BlockSpec(memory_space=pltpu.SMEM)
    vmem = pl.BlockSpec(memory_space=pltpu.VMEM)
    return pl.pallas_call(
        kernel,
        name="scatter_matmul",
        out_shape=jax.ShapeDtypeStruct((dest_blocks, tile_width, feat_width), jnp.bfloat16),
        in_specs=[smem, smem, smem, vmem, vmem],
        out_specs=vmem,
        scratch_shapes=[pltpu.VMEM((dest_blocks + 1, tile_width, feat_width), jnp.float32)],
        cost_estimate=pl.CostEstimate(
            flops=2 * slot_total * tile_width * tile_width * feat_width,
            bytes_accessed=table.size * 2 + tiles.size * 2 + dest_blocks * tile_width * feat_width * 2,
            transcendentals=0,
        ),
        compiler_params=pltpu.CompilerParams(vmem_limit_bytes=40 * 1024 * 1024),
    )(source_ids, target_ids, live_count, table, tiles)


def per_device(features, edge_tiles, tile_src, tile_dst, tile_count, weight, out_bias):
    tiles_here = edge_tiles[0, 0]
    source_ids = tile_src[0, 0]
    target_ids = tile_dst[0, 0]
    live_count = tile_count[0]
    slot_total = tiles_here.shape[0]
    tile_width = tiles_here.shape[-1]
    node_rows, feat_width = features.shape
    group_count = lax.axis_size("row")
    dest_blocks = group_count * node_rows // tile_width
    live_slot = jnp.arange(slot_total, dtype=jnp.int32) < live_count[0]

    table = lax.all_gather(features, "blk", axis=0, tiled=True)

    row_sums = jnp.sum(tiles_here, axis=2, dtype=jnp.float32)
    block_ids = jnp.arange(dest_blocks, dtype=jnp.int32)
    selector = ((target_ids[None, :] == block_ids[:, None]) & live_slot[None, :]).astype(jnp.float32)
    degree_part = jnp.dot(selector, row_sums, precision=lax.Precision.HIGHEST)
    degree_parts = lax.all_to_all(
        degree_part.astype(jnp.bfloat16).reshape(group_count, node_rows), "row", 0, 0
    )
    degree = jnp.sum(degree_parts.astype(jnp.float32), axis=0)
    own_part = jnp.dot(features, weight[:feat_width], preferred_element_type=jnp.float32) + out_bias

    partial = scatter_matmul(
        table.reshape(-1, tile_width, feat_width), tiles_here, source_ids, target_ids, live_count, dest_blocks
    )
    aggregate = lax.psum_scatter(
        partial.reshape(-1, feat_width), "row", scatter_dimension=0, tiled=True
    ).astype(jnp.float32)
    neighbor_mean = (aggregate / jnp.maximum(degree, 1.0)[:, None]).astype(jnp.bfloat16)
    mixed = jnp.dot(neighbor_mean, weight[feat_width:], preferred_element_type=jnp.float32) + own_part
    return jax.nn.relu(mixed).astype(jnp.bfloat16)


def solution(mesh):
    in_specs = (
        P(("row", "blk"), None),
        P("row", "blk", None, None, None),
        P("row", "blk", None),
        P("row", "blk", None),
        P("row", "blk"),
        P(),
        P(),
    )
    return jax.shard_map(
        per_device, mesh=mesh, in_specs=in_specs, out_specs=P(("row", "blk"), None), check_vma=False
    )
```

time: 282 us -> 212 us (0.75)
  matrix products: 61.5 us -> 2.43 us
  waiting for transfers between devices: 143 us -> 162 us
  blocking collectives: 36.3 us -> 18.8 us
  local copies, waits for them, and re-layouts: 23.2 us -> 9.94 us
    dot_general x11 -> x3, matrix products: 61.5 us -> 2.43 us  [the longest x1 1.29 us: per_device(): jnp.dot(neighbor_mean, weight[feat_width:], preferred_element_type=jnp.fl...]
    unnamed x1 -> x0, blocking collectives: 36.3 us -> none
    all_to_all x0 -> x1, blocking collectives: none -> 18.8 us  [per_device(): lax.all_to_all(degree_part.astype(jnp.bfloat16).reshape(group_count, node...]
    reduce_scatter x1, waiting for transfers between devices: 61.5 us -> 79.8 us  [per_device(): lax.psum_scatter(partial.reshape(-1, feat_width), 'row', scatter_dimensio...]
    while x1 -> x0, local copies, waits for them, and re-layouts: 9.77 us -> none  [accumulate(): return lax.fori_loop(0, rounds, one_round, empty)]
    unnamed x14 -> x22, local copies, waits for them, and re-layouts: 12.8 us -> 9.41 us
where the time goes in v1:
time: 212 us; the launch traced here: 211 us
  waiting for transfers between devices  162 us (76%)
  blocking collectives  18.8 us (9%)
  between operations  14.1 us (7%)
  local copies, waits for them, and re-layouts  9.94 us (5%)
  Pallas kernels  2.52 us (1%)
  matrix products  2.43 us (1%)
    all_gather x1, waiting for transfers between devices, per_device(): table = lax.all_gather(features, 'blk', axis=0, tiled=True)  81 us
    reduce_scatter x1, waiting for transfers between devices, per_device(): lax.psum_scatter(partial.reshape(-1, feat_width), 'row', scatter_dimensio...  79.8 us
    all_to_all x1, blocking collectives, per_device(): lax.all_to_all(degree_part.astype(jnp.bfloat16).reshape(group_count, node...  18.8 us
    unnamed x22, local copies, waits for them, and re-layouts  9.41 us
  transfers between devices with their start and end apart: 2, of which 2 were waited for; matrix products, arithmetic and copies ran while one was open for 1% of the time, Pallas kernels for 0%

profile of v1, /device:TPU:6, one launch (start us, length us, event | category | flops | bytes accessed | tf_op | source)
XLA Modules:
  0.0 210.7 jit_solution(16541976957763668319)
XLA Ops:
  6.5 0.0 all-gather.2.cloned.1.call-start
  6.5 0.7 all-gather.2.cloned.1.call-update
  7.3 0.0 reduce-scatter.2.cloned.1.call-start
  7.9 81.0 %all-gather.2.cloned.1.call-done = bf16[8192,512]{1,0:T(8,128)(2,1)} async-done(((bf16[256,512]{1,0:T(8,128)(2,1)}), bf16[8192,512]{1,0:T(8,128)(2,1)}) %all-gather.2.cloned.1.call-update) | async-done | bytes 8388624 | tf_op jit(solution)/shard_map/all_gather | solution.py:79
  89.0 0.0 copy-start.1
  89.0 3.4 %copy-done.1 = bf16[8192,512]{1,0:T(8,128)(2,1)S(1)} copy-done((bf16[8192,512]{1,0:T(8,128)(2,1)S(1)}, bf16[8192,512]{1,0:T(8,128)(2,1)}, u32[]{:S(2)}) %copy-start.1) | copy-done | bytes 8388632
  92.4 1.4 copy-done.2
  93.8 0.0 copy-start.4
  93.8 0.7 copy-done.4
  94.4 0.0 copy-start.6
  94.4 0.7 copy-done.6
  95.1 2.5 %scatter_matmul.1 = bf16[32,128,512]{2,1,0:T(8,128)(2,1)S(1)} custom-call(s32[48]{0:T(128)S(1)} %bitcast.17, s32[48]{0:T(128)S(1)} %bitcast.15, s32[1]{0:T(128)} %bitcast.10.count_ref, bf16[64,128,512]{2,1,0:T(8,128)(2,1)S(1)} %bitcast.13, bf16[48,128,128]{2,1,0:T(8,128)(2,1)S(1)} %bitcast.14), custom_call_target="tpu_custom_call" | custom-call | flops 805306368 | bytes 14155776 | tf_op jit(solution)/shard_map/scatter_matmul/pallas_call | solution.py:51
  97.6 0.0 copy-start
  97.6 1.9 copy-done
  99.5 0.0 copy-start.3
  99.6 0.0 copy-start.5
  99.6 0.0 reduce-scatter.2.cloned.1.call-update
  99.6 0.0 copy-start.7
  99.6 0.0 copy-start.9
  99.6 1.3 copy-done.3
  101.0 0.5 convert_reduce_fusion
  101.4 0.0 copy-done.5
  101.4 0.1 convolution_convert_fusion
  101.6 0.5 broadcast.9
  102.1 0.7 reduce.1
  102.8 18.8 %all_to_all.10 = bf16[16,2,128]{2,1,0:T(2,128)(2,1)S(1)} all-to-all(bf16[16,2,128]{2,1,0:T(2,128)(2,1)S(1)} %reshape.22), channel_id=1, replica_groups=mesh['row'=16,'blk'=32] {'row'}, dimensions={0} | all-to-all | bytes 16384 | tf_op jit(solution)/shard_map/all_to_all | solution.py:85
  121.7 79.8 %reduce-scatter.2.cloned.1.call-done = bf16[256,512]{1,0:T(8,128)(2,1)} async-done(((bf16[4096,512]{1,0:T(8,128)(2,1)}), bf16[256,512]{1,0:T(8,128)(2,1)}) %reduce-scatter.2.cloned.1.call-update) | async-done | bytes 262160 | tf_op jit(solution)/shard_map/reduce_scatter | solution.py:94
  201.5 0.0 copy-done.8
  201.5 1.3 fusion.4
  202.8 0.0 copy-done.7
  202.8 0.0 copy-done.9
  202.8 1.0 fusion.2
  (8 shorter events, 0.1 us)
Async XLA Ops:
  6.5 82.4 %all-gather.2.cloned.1.call-start = ((), (), s32[]{:S(2)}) async-start(), calls=%async_computation.2 | async-start | bytes 8650752 | tf_op jit(solution)/shard_map/all_gather | solution.py:79
  7.3 194.3 %reduce-scatter.2.cloned.1.call-start = ((), (), s32[]{:S(2)}) async-start(), calls=%async_computation.3 | async-start | bytes 4456448 | tf_op jit(solution)/shard_map/reduce_scatter | solution.py:94
  89.0 3.4 %copy-start.1 = (bf16[8192,512]{1,0:T(8,128)(2,1)S(1)}, bf16[8192,512]{1,0:T(8,128)(2,1)}, u32[]{:S(2)}) copy-start(bf16[8192,512]{1,0:T(8,128)(2,1)} %all-gather.2.cloned.1.call-done) | copy-start | bytes 25165828
  92.4 1.4 copy-start.2
  93.8 0.7 copy-start.4
  94.4 0.7 copy-start.6
  97.6 1.9 copy-start
  99.5 1.4 copy-start.3
  99.6 1.9 copy-start.5
  99.6 102.0 %copy-start.8 = (bf16[1024,512]{1,0:T(8,128)(2,1)S(1)}, bf16[1024,512]{1,0:T(8,128)(2,1)}, u32[]{:S(2)}) copy-start(bf16[1024,512]{1,0:T(8,128)(2,1)} %param.12) | copy-start | bytes 3145732
  99.6 103.3 %copy-start.7 = (bf16[256,512]{1,0:T(8,128)(2,1)S(1)}, bf16[256,512]{1,0:T(8,128)(2,1)}, u32[]{:S(2)}) copy-start(bf16[256,512]{1,0:T(8,128)(2,1)} %param.7) | copy-start | bytes 786436
  99.6 103.3 %copy-start.9 = (f32[512]{0:T(512)S(1)}, f32[512]{0:T(512)}, u32[]{:S(2)}) copy-start(f32[512]{0:T(512)} %param.13) | copy-start | bytes 6148
Sparse Core Ops, SparseCore 0:
  9.5 79.4 all-gather.1
  99.7 101.7 reduce-scatter.1
